TPU v7x, 32 devices: a whole 2x2x4 slice. The times are simulated.
32 devices in a mesh: tok: 4 (over x, core), vocab: 8 (over z, y).
Axes of the slice: x: 2, y: 2, z: 4, core: 2. Of those that a mesh axis runs over, the one named last changes fastest.
Arguments:
- hidden_states: bfloat16 [512, 3584], P('tok'), may hold values from -6 to 6, as said below
- hidden_tangent: bfloat16 [512, 3584], P('tok'), may hold values from -6 to 6
- buckets: int32 [512], P('tok'), may hold values from 0 to 7
- head_weight: bfloat16 [3584, 5120], P(None, 'vocab')
Outputs:
- hidden_cotangent: bfloat16 [3584, 512], P('vocab', 'tok')
- weight_gradient: bfloat16 [3584, 5120], P('tok', 'vocab')
Inputs may be any that keep to these rules, and one draw needn't show every extreme that they name: `hidden_states`: hidden states of order one.
All inputs are finite; a program needn't handle non-finite values.
Results may differ from a plain program's by a relative error of at most 0.0107.
Values may be sent and summed in bfloat16 or wider, within the bound.
A program may use at most 64 MiB of HBM per device.

v0:
```python
import jax
import jax.numpy as jnp
from jax import lax
from jax.sharding import PartitionSpec as P

TOK_DEV = 128
BUCKETS = 8


def local(hidden_states, hidden_tangent, buckets, head_weight):
    logits = jnp.dot(hidden_states, head_weight, preferred_element_type=jnp.float32)
    tangent = jnp.dot(hidden_tangent, head_weight, preferred_element_type=jnp.float32)
    peak = lax.pmax(jnp.max(logits, axis=1), "vocab")
    expo = jnp.exp(logits - peak[:, None])
    total = lax.psum(jnp.sum(expo, axis=1), "vocab")
    probs = expo / total[:, None]
    mean = lax.psum(jnp.sum(probs * tangent, axis=1), "vocab")
    scale = 0.25 * jnp.exp2(buckets.astype(jnp.float32) * (3.0 / (BUCKETS - 1)))
    grads = (scale[:, None] * probs * (tangent - mean[:, None])).astype(jnp.bfloat16)
    width = head_weight.shape[0]
    cotan = lax.psum_scatter(
        lax.dot_general(
            head_weight, grads, (((1,), (1,)), ((), ())), preferred_element_type=jnp.float32
        ),
        "vocab",
        scatter_dimension=0,
        tiled=True,
    )
    hidden_cotangent = cotan.astype(jnp.bfloat16)
    feature_rows = width // lax.axis_size("tok")
    column_start = lax.axis_index("tok") * feature_rows
    pieces = (
        lax.all_gather(hidden_states, "tok", axis=0, tiled=True),
        lax.all_gather(grads, "tok", axis=0, tiled=True),
    )
    columns = lax.dynamic_slice_in_dim(pieces[0], column_start, feature_rows, 1)
    blocks_h = columns.reshape(-1, TOK_DEV, feature_rows)
    blocks_g = pieces[1].reshape(-1, TOK_DEV, pieces[1].shape[1])
    partial_terms = jnp.einsum(
        "kti,ktv->kiv", blocks_h, blocks_g, preferred_element_type=jnp.float32
    ).astype(jnp.bfloat16)
    summed = jnp.sum(partial_terms.astype(jnp.float32), axis=0)
    return (hidden_cotangent, summed.astype(jnp.bfloat16))


def solution(mesh):
    return jax.shard_map(
        local,
        mesh=mesh,
        in_specs=(P("tok", None), P("tok", None), P("tok"), P(None, "vocab")),
        out_specs=(P("vocab", "tok"), P("tok", "vocab")),
        check_vma=False,
    )
```

profile of v0, /device:TPU:0, one launch (start us, length us, event | category | flops | bytes accessed | tf_op | source)
XLA Modules:
  0.0 158.0 jit_solution(476871489584601557)
XLA Ops:
  8.0 0.0 copy-start
  8.0 0.0 reduce-scatter.4.cloned.1.call-start
  8.1 0.7 exponential_multiply_fusion
  8.8 3.6 %fusion.2 = (f32[128]{0:T(128)S(1)}, f32[128,640]{1,0:T(8,128)S(1)}) fusion(bf16[128,3584]{1,0:T(8,128)(2,1)} %param.4, bf16[3584,640]{1,0:T(8,128)(2,1)} %param.7), kind=kOutput, calls=%fused_computation.9 | convolution fusion | flops 587284352 | bytes 5833216 | tf_op jit(solution)/shard_map/dot_general | solution.py:11
  12.3 23.2 %pmax.7 = f32[128]{0:T(128)S(1)} all-reduce(f32[128]{0:T(128)S(1)} %get-tuple-element.8), channel_id=1, replica_groups=mesh['tok'=4,'vocab'=8] {'vocab'}, use_global_device_ids=true, to_apply=%region_1.0 | all-reduce | flops 128 | bytes 1024 | tf_op jit(solution)/shard_map/pmax | solution.py:13
  35.5 0.2 fusion.1
  35.7 17.1 %psum.14 = f32[128]{0:T(128)S(1)} all-reduce(f32[128]{0:T(128)S(1)} %fusion.1), channel_id=1, replica_groups=mesh['tok'=4,'vocab'=8] {'vocab'}, use_global_device_ids=true, to_apply=%region_3.0 | all-reduce | flops 128 | bytes 1024 | tf_op jit(solution)/shard_map/psum | solution.py:15
  52.8 0.0 copy-done
  52.8 3.3 %multiply_reduce_fusion = (f32[128]{0:T(128)S(1)}, f32[128,640]{1,0:T(8,128)S(1)}) fusion(f32[128]{0:T(128)S(1)} %psum.14, f32[128,640]{1,0:T(8,128)S(1)} %get-tuple-element.9, f32[128]{0:T(128)S(1)} %pmax.7, bf16[128,3584]{1,0:T(8,128)(2,1)S(1)} %copy-done, bf16[3584,640]{1,0:T(8,128)(2,1)} %param.7), kind=kOutput, calls=%fused_computation.3 | convolution fusion | flops 587530112 | bytes 6161920 | tf_op jit(solution)/shard_map/dot_general | solution.py:12
  56.1 19.1 %psum.15 = f32[128]{0:T(128)S(1)} all-reduce(f32[128]{0:T(128)S(1)} %get-tuple-element.10), channel_id=1, replica_groups=mesh['tok'=4,'vocab'=8] {'vocab'}, use_global_device_ids=true, to_apply=%region_5.0 | all-reduce | flops 128 | bytes 1024 | tf_op jit(solution)/shard_map/psum | solution.py:17
  75.2 0.2 multiply_convert_fusion
  75.4 3.9 %convolution_bitcast_fusion = f32[3584,128]{0,1:T(8,128)S(1)} fusion(bf16[128,640]{1,0:T(8,128)(2,1)S(1)} %multiply_convert_fusion, bf16[3584,640]{1,0:T(8,128)(2,1)} %param.7), kind=kOutput, calls=%fused_computation | convolution fusion | flops 587202560 | bytes 6586368 | tf_op jit(solution)/shard_map/dot_general | solution.py:22
  79.3 1.7 %copy.12 = f32[3584,128]{1,0:T(8,128)} copy(f32[3584,128]{0,1:T(8,128)S(1)} %convolution_bitcast_fusion) | data formatting | bytes 3670016
  81.0 0.0 reduce-scatter.4.cloned.1.call-update
  81.0 0.0 all-gather.2.cloned.1.call-start
  81.0 0.5 all-gather.2.cloned.1.call-update
  81.6 7.9 %all_gather.7 = bf16[512,640]{1,0:T(8,128)(2,1)S(1)} all-gather(bf16[128,640]{1,0:T(8,128)(2,1)S(1)} %multiply_convert_fusion), channel_id=1, replica_groups=mesh['tok'=4,'vocab'=8] {'tok'}, dimensions={0}, use_global_device_ids=true | all-gather | bytes 819200 | tf_op jit(solution)/shard_map/all_gather | solution.py:34
  89.5 55.5 %reduce-scatter.4.cloned.1.call-done = f32[448,128]{1,0:T(8,128)} async-done(((f32[3584,128]{1,0:T(8,128)}), f32[448,128]{1,0:T(8,128)}) %reduce-scatter.4.cloned.1.call-update) | async-done | bytes 229392
  145.0 1.0 copy.13
  146.1 0.8 copy.10
  146.8 0.0 all-gather.2.cloned.1.call-done
  146.8 1.3 constant_dynamic-slice_fusion
  148.1 2.4 %convert_reduce_fusion = bf16[896,640]{1,0:T(8,128)(2,1)} fusion(bf16[4,128,896]{2,1,0:T(8,128)(2,1)S(1)} %bitcast.13, bf16[4,128,640]{2,1,0:T(8,128)(2,1)S(1)} %bitcast.14), kind=kOutput, calls=%fused_computation.1 | convolution fusion | flops 591216640 | bytes 2719744 | tf_op jit(solution)/shard_map/kti,ktv->kiv/dot_general | solution.py:39
Async XLA Ops:
  8.0 44.8 %copy-start = (bf16[128,3584]{1,0:T(8,128)(2,1)S(1)}, bf16[128,3584]{1,0:T(8,128)(2,1)}, u32[]{:S(2)}) copy-start(bf16[128,3584]{1,0:T(8,128)(2,1)} %param.5) | copy-start | bytes 2752516
  8.0 137.0 %reduce-scatter.4.cloned.1.call-start = ((), (), s32[]{:S(2)}) async-start(), calls=%async_computation.2 | async-start | bytes 2064384
  81.0 65.9 %all-gather.2.cloned.1.call-start = ((), (), s32[]{:S(2)}) async-start(), calls=%async_computation.1 | async-start | bytes 4587520 | tf_op jit(solution)/shard_map/all_gather | solution.py:33
Sparse Core Ops, SparseCore 0:
  81.1 63.8 reduce-scatter.3
Sparse Core Ops, SparseCore 1:
  83.0 28.6 all-gather.1
where the time goes:
time: 158 us
  blocking collectives  67.4 us (43%)
  waiting for transfers between devices  56.1 us (36%)
  between operations  15.5 us (10%)
  matrix products  13.1 us (8%)
  local copies, waits for them, and re-layouts  4.77 us (3%)
    unnamed x3, waiting for transfers between devices  56.1 us
    pmax x1, blocking collectives, local(): peak = lax.pmax(jnp.max(logits, axis=1), 'vocab')  23.2 us
    psum x1, blocking collectives, local(): mean = lax.psum(jnp.sum(probs * tangent, axis=1), 'vocab')  19.1 us
    psum x1, blocking collectives, local(): total = lax.psum(jnp.sum(expo, axis=1), 'vocab')  17.1 us
    all_gather x1, blocking collectives, local(): lax.all_gather(grads, 'tok', axis=0, tiled=True)  7.94 us
    dot_general x1, matrix products, local(): lax.dot_general(head_weight, grads, (((1,), (1,)), ((), ())), preferred_e...  3.85 us
    dot_general x1, matrix products, local(): jnp.dot(hidden_states, head_weight, preferred_element_type=jnp.float32)  3.55 us
    unnamed x5, local copies, waits for them, and re-layouts  3.52 us
  transfers between devices with their start and end apart: 2, of which 1 were waited for; matrix products, arithmetic and copies ran while one was open for 1% of the time, Pallas kernels for 0%

commit v1 on v0

--- a/solution.py
+++ b/solution.py
@@ -14,7 +14,9 @@
     expo = jnp.exp(logits - peak[:, None])
     total = lax.psum(jnp.sum(expo, axis=1), "vocab")
     probs = expo / total[:, None]
-    mean = lax.psum(jnp.sum(probs * tangent, axis=1), "vocab")
+    own = jnp.sum(probs * tangent, axis=1)
+    parts = lax.all_gather(own, "vocab")
+    mean = jnp.sum(parts, axis=0)
     scale = 0.25 * jnp.exp2(buckets.astype(jnp.float32) * (3.0 / (BUCKETS - 1)))
     grads = (scale[:, None] * probs * (tangent - mean[:, None])).astype(jnp.bfloat16)
     width = head_weight.shape[0]

time: 158 us -> 158 us (level)
    psum x1 -> x0, blocking collectives: 19.1 us -> none  [local(): mean = lax.psum(jnp.sum(probs * tangent, axis=1), 'vocab')]
    all_gather x0 -> x1, blocking collectives: none -> 18.3 us  [local(): parts = lax.all_gather(own, 'vocab')]
where the time goes in v1:
time: 158 us; the launch traced here: 157 us
  blocking collectives  66.5 us (42%)
  waiting for transfers between devices  56.1 us (36%)
  between operations  15.5 us (10%)
  matrix products  13.1 us (8%)
  local copies, waits for them, and re-layouts  4.77 us (3%)
    unnamed x3, waiting for transfers between devices  56.1 us
    pmax x1, blocking collectives, local(): peak = lax.pmax(jnp.max(logits, axis=1), 'vocab')  23.2 us
    all_gather x1, blocking collectives, local(): parts = lax.all_gather(own, 'vocab')  18.3 us
    psum x1, blocking collectives, local(): total = lax.psum(jnp.sum(expo, axis=1), 'vocab')  17.1 us
    all_gather x1, blocking collectives, local(): lax.all_gather(grads, 'tok', axis=0, tiled=True)  7.94 us
    dot_general x1, matrix products, local(): lax.dot_general(head_weight, grads, (((1,), (1,)), ((), ())), preferred_e...  3.85 us
    dot_general x1, matrix products, local(): jnp.dot(hidden_states, head_weight, preferred_element_type=jnp.float32)  3.55 us
    unnamed x5, local copies, waits for them, and re-layouts  3.52 us
  transfers between devices with their start and end apart: 2, of which 1 were waited for; matrix products, arithmetic and copies ran while one was open for 1% of the time, Pallas kernels for 0%

profile of v1, /device:TPU:0, one launch (start us, length us, event | category | flops | bytes accessed | tf_op | source)
XLA Modules:
  0.0 157.2 jit_solution(11065419158914338392)
XLA Ops:
  8.0 0.0 copy-start
  8.0 0.0 reduce-scatter.4.cloned.1.call-start
  8.1 0.7 exponential_multiply_fusion
  8.8 3.6 %fusion.2 = (f32[128]{0:T(128)S(1)}, f32[128,640]{1,0:T(8,128)S(1)}) fusion(bf16[128,3584]{1,0:T(8,128)(2,1)} %param.4, bf16[3584,640]{1,0:T(8,128)(2,1)} %param.7), kind=kOutput, calls=%fused_computation.9 | convolution fusion | flops 587284352 | bytes 5833216 | tf_op jit(solution)/shard_map/dot_general | solution.py:11
  12.3 23.2 %pmax.7 = f32[128]{0:T(128)S(1)} all-reduce(f32[128]{0:T(128)S(1)} %get-tuple-element.8), channel_id=1, replica_groups=mesh['tok'=4,'vocab'=8] {'vocab'}, use_global_device_ids=true, to_apply=%region_1.0 | all-reduce | flops 128 | bytes 1024 | tf_op jit(solution)/shard_map/pmax | solution.py:13
  35.5 0.2 fusion.1
  35.7 17.1 %psum.7 = f32[128]{0:T(128)S(1)} all-reduce(f32[128]{0:T(128)S(1)} %fusion.1), channel_id=1, replica_groups=mesh['tok'=4,'vocab'=8] {'vocab'}, use_global_device_ids=true, to_apply=%region_3.0 | all-reduce | flops 128 | bytes 1024 | tf_op jit(solution)/shard_map/psum | solution.py:15
  52.8 0.0 copy-done
  52.8 3.3 %multiply_reduce_fusion = (f32[128]{0:T(128)S(1)}, f32[128,640]{1,0:T(8,128)S(1)}) fusion(f32[128]{0:T(128)S(1)} %psum.7, f32[128,640]{1,0:T(8,128)S(1)} %get-tuple-element.9, f32[128]{0:T(128)S(1)} %pmax.7, bf16[128,3584]{1,0:T(8,128)(2,1)S(1)} %copy-done, bf16[3584,640]{1,0:T(8,128)(2,1)} %param.7), kind=kOutput, calls=%fused_computation.3 | convolution fusion | flops 587530112 | bytes 6161920 | tf_op jit(solution)/shard_map/dot_general | solution.py:12
  56.1 18.3 %all-gather.1 = f32[8,1,128]{2,1,0:T(1,128)S(1)} all-gather(f32[1,1,128]{2,1,0:T(1,128)S(1)} %bitcast.16), channel_id=2, replica_groups=mesh['tok'=4,'vocab'=8] {'vocab'}, dimensions={0}, use_global_device_ids=true | all-gather | bytes 4608 | tf_op jit(solution)/shard_map/all_gather | solution.py:18
  74.4 0.2 multiply_convert_fusion
  74.6 3.9 %convolution_bitcast_fusion = f32[3584,128]{0,1:T(8,128)S(1)} fusion(bf16[128,640]{1,0:T(8,128)(2,1)S(1)} %multiply_convert_fusion, bf16[3584,640]{1,0:T(8,128)(2,1)} %param.7), kind=kOutput, calls=%fused_computation | convolution fusion | flops 587202560 | bytes 6586368 | tf_op jit(solution)/shard_map/dot_general | solution.py:24
  78.4 1.7 %copy.12 = f32[3584,128]{1,0:T(8,128)} copy(f32[3584,128]{0,1:T(8,128)S(1)} %convolution_bitcast_fusion) | data formatting | bytes 3670016
  80.1 0.0 reduce-scatter.4.cloned.1.call-update
  80.2 0.0 all-gather.4.cloned.1.call-start
  80.2 0.5 all-gather.4.cloned.1.call-update
  80.7 7.9 %all_gather.15 = bf16[512,640]{1,0:T(8,128)(2,1)S(1)} all-gather(bf16[128,640]{1,0:T(8,128)(2,1)S(1)} %multiply_convert_fusion), channel_id=1, replica_groups=mesh['tok'=4,'vocab'=8] {'tok'}, dimensions={0}, use_global_device_ids=true | all-gather | bytes 819200 | tf_op jit(solution)/shard_map/all_gather | solution.py:36
  88.7 55.6 %reduce-scatter.4.cloned.1.call-done = f32[448,128]{1,0:T(8,128)} async-done(((f32[3584,128]{1,0:T(8,128)}), f32[448,128]{1,0:T(8,128)}) %reduce-scatter.4.cloned.1.call-update) | async-done | bytes 229392
  144.3 1.0 copy.13
  145.3 0.8 copy.10
  146.1 0.0 all-gather.4.cloned.1.call-done
  146.1 1.3 constant_dynamic-slice_fusion
  147.4 2.4 %convert_reduce_fusion = bf16[896,640]{1,0:T(8,128)(2,1)} fusion(bf16[4,128,896]{2,1,0:T(8,128)(2,1)S(1)} %bitcast.14, bf16[4,128,640]{2,1,0:T(8,128)(2,1)S(1)} %bitcast.15), kind=kOutput, calls=%fused_computation.1 | convolution fusion | flops 591216640 | bytes 2719744 | tf_op jit(solution)/shard_map/kti,ktv->kiv/dot_general | solution.py:41
  (1 shorter events, 0.0 us)
Async XLA Ops:
  8.0 44.8 %copy-start = (bf16[128,3584]{1,0:T(8,128)(2,1)S(1)}, bf16[128,3584]{1,0:T(8,128)(2,1)}, u32[]{:S(2)}) copy-start(bf16[128,3584]{1,0:T(8,128)(2,1)} %param.5) | copy-start | bytes 2752516
  8.0 136.3 %reduce-scatter.4.cloned.1.call-start = ((), (), s32[]{:S(2)}) async-start(), calls=%async_computation.2 | async-start | bytes 2064384
  80.2 65.9 %all-gather.4.cloned.1.call-start = ((), (), s32[]{:S(2)}) async-start(), calls=%async_computation.1 | async-start | bytes 4587520 | tf_op jit(solution)/shard_map/all_gather | solution.py:35
Sparse Core Ops, SparseCore 0:
  80.3 63.9 reduce-scatter.3
Sparse Core Ops, SparseCore 1:
  82.2 28.6 all-gather.3

commit v2 on v0

--- a/solution.py
+++ b/solution.py
@@ -5,6 +5,23 @@
 
 TOK_DEV = 128
 BUCKETS = 8
+
+
+def in_order(blocks, dim):
+    blocks = jnp.moveaxis(blocks, 0, dim)
+    shape = blocks.shape
+    return blocks.reshape(*shape[:dim], shape[dim] * shape[dim + 1], *shape[dim + 2 :])
+
+
+def gather_around(value, axis, dim):
+    devices = lax.axis_size(axis)
+    ahead = [(i, (i + 1) % devices) for i in range(devices)]
+    blocks = [value]
+    while len(blocks) < devices:
+        blocks.append(lax.ppermute(blocks[-1], axis, ahead))
+    mine = lax.axis_index(axis)
+    blocks = jnp.stack(blocks)[(mine - jnp.arange(devices)) % devices]
+    return in_order(blocks, dim)
 
 
 def local(hidden_states, hidden_tangent, buckets, head_weight):
@@ -31,7 +48,7 @@
     column_start = lax.axis_index("tok") * feature_rows
     pieces = (
         lax.all_gather(hidden_states, "tok", axis=0, tiled=True),
-        lax.all_gather(grads, "tok", axis=0, tiled=True),
+        gather_around(grads, "tok", 0),
     )
     columns = lax.dynamic_slice_in_dim(pieces[0], column_start, feature_rows, 1)
     blocks_h = columns.reshape(-1, TOK_DEV, feature_rows)

time: 158 us -> 158 us (level)
  blocking collectives: 67.4 us -> 59.4 us
  waiting for transfers between devices: 56.1 us -> 61.7 us
    ppermute x0 -> x3, waiting for transfers between devices: none -> 17.5 us  [gather_around(): blocks.append(lax.ppermute(blocks[-1], axis, ahead))]
    unnamed x3, waiting for transfers between devices: 56.1 us -> 44.2 us
    all_gather x1 -> x0, blocking collectives: 7.94 us -> none  [local(): lax.all_gather(grads, 'tok', axis=0, tiled=True)]
  transfers between devices with their start and end apart: 2 -> 5, of which waited for: 1 -> 4; matrix products, arithmetic and copies ran while one was open for 1% -> 2% of each run, Pallas kernels for 0% -> 0%
where the time goes in v2:
time: 158 us
  waiting for transfers between devices  61.7 us (39%)
  blocking collectives  59.4 us (38%)
  between operations  15.5 us (10%)
  matrix products  13.1 us (8%)
  local copies, waits for them, and re-layouts  5.43 us (3%)
  starting transfers between devices  1.61 us (1%)
    unnamed x3, waiting for transfers between devices  44.2 us
    pmax x1, blocking collectives, local(): peak = lax.pmax(jnp.max(logits, axis=1), 'vocab')  23.2 us
    psum x1, blocking collectives, local(): mean = lax.psum(jnp.sum(probs * tangent, axis=1), 'vocab')  19.1 us
    ppermute x3, waiting for transfers between devices, gather_around(): blocks.append(lax.ppermute(blocks[-1], axis, ahead))  17.5 us
    psum x1, blocking collectives, local(): total = lax.psum(jnp.sum(expo, axis=1), 'vocab')  17.1 us
    dot_general x1, matrix products, local(): lax.dot_general(head_weight, grads, (((1,), (1,)), ((), ())), preferred_e...  3.85 us
    dot_general x1, matrix products, local(): jnp.dot(hidden_states, head_weight, preferred_element_type=jnp.float32)  3.55 us
    unnamed x5, local copies, waits for them, and re-layouts  3.52 us
  transfers between devices with their start and end apart: 5, of which 4 were waited for; matrix products, arithmetic and copies ran while one was open for 2% of the time, Pallas kernels for 0%

profile of v2, /device:TPU:0, one launch (start us, length us, event | category | flops | bytes accessed | tf_op | source)
XLA Modules:
  0.0 158.0 jit_solution(12264140219183082992)
XLA Ops:
  8.0 0.0 copy-start
  8.0 0.0 reduce-scatter.4.cloned.1.call-start
  8.1 0.7 exponential_multiply_fusion
  8.8 3.6 %fusion.4 = (f32[128]{0:T(128)S(1)}, f32[128,640]{1,0:T(8,128)S(1)}) fusion(bf16[128,3584]{1,0:T(8,128)(2,1)} %param.4, bf16[3584,640]{1,0:T(8,128)(2,1)} %param.7), kind=kOutput, calls=%fused_computation.18 | convolution fusion | flops 587284352 | bytes 5833216 | tf_op jit(solution)/shard_map/dot_general | solution.py:28
  12.3 23.2 %pmax.7 = f32[128]{0:T(128)S(1)} all-reduce(f32[128]{0:T(128)S(1)} %get-tuple-element.8), channel_id=1, replica_groups=mesh['tok'=4,'vocab'=8] {'vocab'}, use_global_device_ids=true, to_apply=%region_1.0 | all-reduce | flops 128 | bytes 1024 | tf_op jit(solution)/shard_map/pmax | solution.py:30
  35.5 0.2 fusion.1
  35.7 17.1 %psum.14 = f32[128]{0:T(128)S(1)} all-reduce(f32[128]{0:T(128)S(1)} %fusion.1), channel_id=1, replica_groups=mesh['tok'=4,'vocab'=8] {'vocab'}, use_global_device_ids=true, to_apply=%region_3.0 | all-reduce | flops 128 | bytes 1024 | tf_op jit(solution)/shard_map/psum | solution.py:32
  52.8 0.0 copy-done
  52.8 3.3 %multiply_reduce_fusion = (f32[128]{0:T(128)S(1)}, f32[128,640]{1,0:T(8,128)S(1)}) fusion(f32[128]{0:T(128)S(1)} %psum.14, f32[128,640]{1,0:T(8,128)S(1)} %get-tuple-element.9, f32[128]{0:T(128)S(1)} %pmax.7, bf16[128,3584]{1,0:T(8,128)(2,1)S(1)} %copy-done, bf16[3584,640]{1,0:T(8,128)(2,1)} %param.7), kind=kOutput, calls=%fused_computation.5 | convolution fusion | flops 587530112 | bytes 6161920 | tf_op jit(solution)/shard_map/dot_general | solution.py:29
  56.1 19.1 %psum.15 = f32[128]{0:T(128)S(1)} all-reduce(f32[128]{0:T(128)S(1)} %get-tuple-element.10), channel_id=1, replica_groups=mesh['tok'=4,'vocab'=8] {'vocab'}, use_global_device_ids=true, to_apply=%region_5.0 | all-reduce | flops 128 | bytes 1024 | tf_op jit(solution)/shard_map/psum | solution.py:34
  75.2 0.2 multiply_convert_fusion
  75.4 3.9 %convolution_bitcast_fusion = f32[3584,128]{0,1:T(8,128)S(1)} fusion(bf16[128,640]{1,0:T(8,128)(2,1)S(1)} %multiply_convert_fusion, bf16[3584,640]{1,0:T(8,128)(2,1)} %param.7), kind=kOutput, calls=%fused_computation.1 | convolution fusion | flops 587202560 | bytes 6586368 | tf_op jit(solution)/shard_map/dot_general | solution.py:39
  79.3 1.7 %copy.12 = f32[3584,128]{1,0:T(8,128)} copy(f32[3584,128]{0,1:T(8,128)S(1)} %convolution_bitcast_fusion) | data formatting | bytes 3670016
  81.0 0.0 reduce-scatter.4.cloned.1.call-update
  81.0 0.0 all-gather.2.cloned.1.call-start
  81.0 0.5 all-gather.2.cloned.1.call-update
  81.6 0.1 collective-permute-start
  81.6 4.7 %collective-permute-done = bf16[128,640]{1,0:T(8,128)(2,1)S(1)} collective-permute-done((bf16[128,640]{1,0:T(8,128)(2,1)S(1)}, bf16[128,640]{1,0:T(8,128)(2,1)S(1)}, u32[]{:S(2)}, u32[]{:S(2)}) %collective-permute-start) | collective-permute-done | bytes 163872 | tf_op jit(solution)/shard_map/ppermute | solution.py:21
  86.4 0.0 collective-permute-start.1
  86.4 5.9 %collective-permute-done.1 = bf16[128,640]{1,0:T(8,128)(2,1)S(1)} collective-permute-done((bf16[128,640]{1,0:T(8,128)(2,1)S(1)}, bf16[128,640]{1,0:T(8,128)(2,1)S(1)}, u32[]{:S(2)}, u32[]{:S(2)}) %collective-permute-start.1) | collective-permute-done | bytes 163872 | tf_op jit(solution)/shard_map/ppermute | solution.py:21
  92.2 1.5 collective-permute-start.2
  93.7 6.9 %collective-permute-done.2 = bf16[128,640]{1,0:T(8,128)(2,1)S(1)} collective-permute-done((bf16[128,640]{1,0:T(8,128)(2,1)S(1)}, bf16[128,640]{1,0:T(8,128)(2,1)S(1)}, u32[]{:S(2)}, u32[]{:S(2)}) %collective-permute-start.2) | collective-permute-done | bytes 163872 | tf_op jit(solution)/shard_map/ppermute | solution.py:21
  100.6 0.1 pad_maximum_fusion
  100.7 0.7 gather_fusion
  101.4 43.6 %reduce-scatter.4.cloned.1.call-done = f32[448,128]{1,0:T(8,128)} async-done(((f32[3584,128]{1,0:T(8,128)}), f32[448,128]{1,0:T(8,128)}) %reduce-scatter.4.cloned.1.call-update) | async-done | bytes 229392
  145.0 1.0 copy.13
  146.1 0.8 copy.10
  146.8 0.0 all-gather.2.cloned.1.call-done
  146.8 1.3 constant_dynamic-slice_fusion
  148.1 2.4 %convert_reduce_fusion = bf16[896,640]{1,0:T(8,128)(2,1)} fusion(bf16[4,128,896]{2,1,0:T(8,128)(2,1)S(1)} %bitcast.19, bf16[4,128,640]{2,1,0:T(8,128)(2,1)S(1)} %gather_fusion), kind=kOutput, calls=%fused_computation.2 | convolution fusion | flops 591216640 | bytes 2719744 | tf_op jit(solution)/shard_map/kti,ktv->kiv/dot_general | solution.py:56
  (2 shorter events, 0.0 us)
Async XLA Ops:
  8.0 44.8 %copy-start = (bf16[128,3584]{1,0:T(8,128)(2,1)S(1)}, bf16[128,3584]{1,0:T(8,128)(2,1)}, u32[]{:S(2)}) copy-start(bf16[128,3584]{1,0:T(8,128)(2,1)} %param.5) | copy-start | bytes 2752516
  8.0 137.0 %reduce-scatter.4.cloned.1.call-start = ((), (), s32[]{:S(2)}) async-start(), calls=%async_computation.2 | async-start | bytes 2064384
  81.0 65.9 %all-gather.2.cloned.1.call-start = ((), (), s32[]{:S(2)}) async-start(), calls=%async_computation.1 | async-start | bytes 4587520 | tf_op jit(solution)/shard_map/all_gather | solution.py:50
  81.6 4.8 %collective-permute-start = (bf16[128,640]{1,0:T(8,128)(2,1)S(1)}, bf16[128,640]{1,0:T(8,128)(2,1)S(1)}, u32[]{:S(2)}, u32[]{:S(2)}) collective-permute-start(bf16[128,640]{1,0:T(8,128)(2,1)S(1)} %multiply_convert_fusion), channel_id=1, source_target_pairs={{0,8},{8,16},{16,24},{24,0},{1,9},{9,17},{17,25},{25,1},{2,10},{10... | collective-permute-start | bytes 491528 | tf_op jit(solution)/shard_map/ppermute | solution.py:21
  86.4 5.9 %collective-permute-start.1 = (bf16[128,640]{1,0:T(8,128)(2,1)S(1)}, bf16[128,640]{1,0:T(8,128)(2,1)S(1)}, u32[]{:S(2)}, u32[]{:S(2)}) collective-permute-start(bf16[128,640]{1,0:T(8,128)(2,1)S(1)} %collective-permute-done), channel_id=1, source_target_pairs={{0,8},{8,16},{16,24},{24,0},{1,9},{9,17},{17,25},{25,1},{2,10},{10... | collective-permute-start | bytes 491528 | tf_op jit(solution)/shard_map/ppermute | solution.py:21
  92.2 8.4 %collective-permute-start.2 = (bf16[128,640]{1,0:T(8,128)(2,1)S(1)}, bf16[128,640]{1,0:T(8,128)(2,1)S(1)}, u32[]{:S(2)}, u32[]{:S(2)}) collective-permute-start(bf16[128,640]{1,0:T(8,128)(2,1)S(1)} %collective-permute-done.1), channel_id=1, source_target_pairs={{0,8},{8,16},{16,24},{24,0},{1,9},{9,17},{17,25},{25,1},{2,10},{10... | collective-permute-start | bytes 491528 | tf_op jit(solution)/shard_map/ppermute | solution.py:21
Sparse Core Ops, SparseCore 0:
  81.1 63.8 reduce-scatter.3
Sparse Core Ops, SparseCore 1:
  83.0 31.0 all-gather.1
